TPU v7x, 32 devices: a whole 2x2x4 slice. The times are simulated.
32 devices in a mesh: tm: 4 (over z), query: 2 (over y), rec: 4 (over x, core).
Axes of the slice: x: 2, y: 2, z: 4, core: 2. Of those that a mesh axis runs over, the one named last changes fastest.
Arguments:
- frames: bfloat16 [4, 2048, 1024], P('rec', 'tm'), may hold values from -100 to 100
- queries: bfloat16 [4096, 1024], P('query'), may hold values from -10 to 10
- kernel: float32 [33, 4096], P(None, 'query'), may hold values from 0.01 to 0.12
- labels: int32 [4, 2048], P('rec', 'tm'), may hold values from 0 to 4095
- lengths: int32 [4], P('rec'), may hold values from 512 to 2048, as said below
Outputs:
- grad_frames: bfloat16 [4, 2048, 1024], P('rec', 'tm', 'query')
- grad_queries: bfloat16 [4096, 1024], P('query', 'rec')
- grad_kernel: float32 [33, 4096], P(None, 'query')
Inputs may be any that keep to these rules, and one draw needn't show every extreme that they name: `lengths`: each entry counts the valid frames at the start of its recording; at least one recording has all 2048 frames valid.
All inputs are finite; a program needn't handle non-finite values.
Results may differ from a plain program's by a relative error of at most 0.0049.
Values sent between devices are 32-bit elements; how exact they have to be, the bound alone decides.
A program may use at most 64 MiB of HBM per device.

v0:
```python
import math
import jax
import jax.numpy as jnp
from jax import lax
from jax.sharding import PartitionSpec as P


def merged(x, axis, combine):
    everything = jax.tree.map(lambda part: lax.all_gather(part, axis), x)
    first = jax.tree.map(lambda part: part[0], everything)

    def step(k, so_far):
        return combine(so_far, jax.tree.map(lambda part: part[k], everything))

    return lax.fori_loop(1, lax.axis_size(axis), step, first)


def with_halo(x, sides, width):
    for axis, dim in sides:
        peers, length = (lax.axis_size(axis), x.shape[dim])
        up = [(i, (i + 1) % peers) for i in range(peers - 1)]
        down = [(j, i) for i, j in up]
        last = lax.slice_in_dim(x, length - width, length, axis=dim)
        first = lax.slice_in_dim(x, 0, width, axis=dim)
        before = lax.ppermute(last, axis, up)
        after = lax.ppermute(first, axis, down)
        x = jnp.concatenate([before, x, after], axis=dim)
    return x


def tap_sum(kernel, padded, row_count, flipped):
    tap_count = kernel.shape[0]
    running = jnp.zeros((row_count, padded.shape[1]), jnp.float32)
    for offset in range(tap_count):
        begin_row = tap_count - 1 - offset if flipped else offset
        running = running + kernel[offset][None, :] * padded[begin_row : begin_row + row_count]
    return running


def combine_stats(first_pair, second_pair):
    top_value = jnp.maximum(first_pair[0], second_pair[0])
    total_value = first_pair[1] * jnp.exp(first_pair[0] - top_value) + second_pair[1] * jnp.exp(
        second_pair[0] - top_value
    )
    return (top_value, total_value)


def row_softmax(smooth):
    local_top = jnp.max(smooth, axis=1)
    local_total = jnp.sum(jnp.exp(smooth - local_top[:, None]), axis=1)
    top_value, total_value = merged((local_top, local_total), "query", combine_stats)
    return jnp.exp(smooth - top_value[:, None]) / total_value[:, None]


def per_device(frames, queries, kernel, labels, lengths):
    frame_rows = frames[0]
    label_ids = labels[0]
    length_now = lengths[0]
    row_count = frame_rows.shape[0]
    query_count = queries.shape[0]
    width = frame_rows.shape[1]
    tap_count = kernel.shape[0]
    rim_width = tap_count // 2
    logit_scale = 10.0 / math.sqrt(width)
    frame_start = lax.axis_index("tm") * row_count
    is_valid = frame_start + jnp.arange(row_count, dtype=jnp.int32) < length_now
    query_start = lax.axis_index("query") * query_count
    query_ids = query_start + jnp.arange(query_count, dtype=jnp.int32)
    scores = (
        lax.dot_general(
            frame_rows, queries, (((1,), (1,)), ((), ())), preferred_element_type=jnp.float32
        )
        * logit_scale
    )
    scores = jnp.where(is_valid[:, None], scores, 0.0)
    wide = with_halo(scores, (("tm", 0),), 2 * rim_width)
    label_pad = with_halo(label_ids, (("tm", 0),), rim_width)
    ext_rows = row_count + 2 * rim_width
    ext_frames = frame_start - rim_width + jnp.arange(ext_rows, dtype=jnp.int32)
    ext_valid = (ext_frames >= 0) & (ext_frames < length_now)
    smooth = tap_sum(kernel, wide, ext_rows, False)
    softmax_out = row_softmax(smooth)
    positive = (label_pad[:, None] == query_ids[None, :]).astype(jnp.float32)
    grad_pad = jnp.where(ext_valid[:, None], softmax_out - positive, 0.0)
    map_grad = grad_pad[rim_width : rim_width + row_count]
    padded = wide[rim_width : rim_width + row_count + 2 * rim_width]
    score_grad = tap_sum(kernel, grad_pad, row_count, True)
    score_grad = jnp.where(is_valid[:, None], score_grad, 0.0).astype(jnp.bfloat16)
    frame_part = jnp.dot(score_grad, queries, preferred_element_type=jnp.float32)
    frame_sum = lax.psum_scatter(frame_part, "query", scatter_dimension=1, tiled=True)
    grad_frames = (frame_sum * logit_scale).astype(jnp.bfloat16)[None]
    query_part = lax.dot_general(
        score_grad, frame_rows, (((0,), (0,)), ((), ())), preferred_element_type=jnp.float32
    )
    kernel_part = jnp.stack(
        [
            jnp.sum(map_grad * padded[offset : offset + row_count], axis=0)
            for offset in range(tap_count)
        ]
    )
    query_whole, grad_kernel = lax.psum((query_part, kernel_part), ("tm", "rec"))
    col_count = width // lax.axis_size("rec")
    query_cols = lax.dynamic_slice_in_dim(
        query_whole, lax.axis_index("rec") * col_count, col_count, 1
    )
    grad_queries = (query_cols * logit_scale).astype(jnp.bfloat16)
    return (grad_frames, grad_queries, grad_kernel)


def solution(mesh):
    in_specs = (P("rec", "tm", None), P("query", None), P(None, "query"), P("rec", "tm"), P("rec"))
    out_specs = (P("rec", "tm", "query"), P("query", "rec"), P(None, "query"))
    return jax.shard_map(
        per_device, mesh=mesh, in_specs=in_specs, out_specs=out_specs, check_vma=False
    )
```

profile of v0, /device:TPU:0, one launch (start us, length us, event | category | flops | bytes accessed | tf_op | source)
XLA Modules:
  0.0 326.1 jit_solution(487026478341481205)
XLA Ops:
  8.1 0.8 slice_bitcast_fusion.1
  8.9 4.9 %collective-permute-start.2 = (s32[16]{0:T(128)S(1)}, s32[16]{0:T(128)S(1)}, u32[]{:S(2)}, u32[]{:S(2)}) collective-permute-start(s32[16]{0:T(128)S(1)} %get-tuple-element.101), channel_id=1, source_target_pairs={{0,8},{8,16},{16,24},{1,9},{9,17},{17,25},{2,10},{10,18},{18,26},{... | collective-permute-start | bytes 200 | tf_op jit(solution)/shard_map/ppermute | solution.py:25
  13.8 1.3 collective-permute-start.3
  15.8 4.6 %multiply_select_fusion = f32[512,2048]{1,0:T(8,128)S(1)} fusion(bf16[2048,1024]{1,0:T(8,128)(2,1)} %param.6, pred[512]{0:T(512)(128)(4,1)S(1)} %add_compare_fusion, bf16[1,512,1024]{2,1,0:T(8,128)(2,1)S(1)} %copy-done), kind=kOutput, calls=%fused_computation.265 | convolution fusion | flops 2149580800 | bytes 9437696 | tf_op jit(solution)/shard_map/dot_general | solution.py:70
  20.5 2.0 copy-done.3
  22.5 4.6 %collective-permute-start = (f32[32,2048]{1,0:T(8,128)S(1)}, f32[32,2048]{1,0:T(8,128)S(1)}, u32[]{:S(2)}, u32[]{:S(2)}) collective-permute-start(f32[32,2048]{1,0:T(8,128)S(1)} %get-tuple-element.66), channel_id=1, source_target_pairs={{0,8},{8,16},{16,24},{1,9},{9,17},{17,25},{2,10},{10,18},{18,26},{... | collective-permute-start | bytes 786440 | tf_op jit(solution)/shard_map/ppermute | solution.py:25
  27.0 1.3 collective-permute-start.1
  28.6 0.6 dynamic-slice
  29.9 2.1 collective-permute-done
  32.0 4.1 %collective-permute-done.1 = f32[32,2048]{1,0:T(8,128)S(1)} collective-permute-done((f32[32,2048]{1,0:T(8,128)S(1)}, f32[32,2048]{1,0:T(8,128)S(1)}, u32[]{:S(2)}, u32[]{:S(2)}) %collective-permute-start.1) | collective-permute-done | bytes 262176 | tf_op jit(solution)/shard_map/ppermute | solution.py:26
  36.1 2.8 pad_maximum_fusion.2
  38.9 22.3 %fusion.172 = (f32[544]{0:T(1024)S(1)}, f32[544,2048]{1,0:T(8,128)S(1)}) fusion(f32[32,2048]{1,0:T(8,128)S(1)} %collective-permute-done.1, f32[512,2048]{1,0:T(8,128)S(1)} %copy-done.4, f32[2048]{0:T(1024)S(1)} %bitcast.110, f32[576,2048]{1,0:T(8,128)S(1)} %pad_maximum_fusion.2, f32[2048]{0:T(1024)S(1)} %bitcast.112, f32[2048]{0:T(1024)S(1)} %bitcast.116, ...), kind=kLoop, calls=%fused_computation.285 | loop fusion | flops 75759072 | bytes 147597440 | tf_op jit(solution)/shard_map/reduce_max | solution.py:49
  61.2 2.0 copy-done.6
  63.2 0.7 exponential_reduce_fusion
  64.0 0.3 dynamic-update-slice
  64.3 0.3 dynamic-update-slice.1
  64.6 8.1 %all-reduce.3 = (f32[1088]{0:T(1024)S(1)}, f32[1088]{0:T(1024)S(1)}) all-reduce(f32[1088]{0:T(1024)S(1)} %dynamic-update-slice.1, f32[1088]{0:T(1024)S(1)} %dynamic-update-slice), channel_id=3, replica_groups=mesh['tm'=4,'query'=2,'rec'=4] {'query'}, use_global_device_ids=true, to_apply=%add.1 | all-reduce | flops 2176 | bytes 17408
  72.7 3.1 subtract_select_fusion
  75.9 18.4 %fusion.132 = bf16[512,2048]{1,0:T(8,128)(2,1)} fusion(f32[544,2048]{1,0:T(8,128)S(1)} %subtract_select_fusion, f32[2048]{0:T(1024)S(1)} %bitcast.111, f32[2048]{0:T(1024)S(1)} %bitcast.113, f32[2048]{0:T(1024)S(1)} %bitcast.117, f32[2048]{0:T(1024)S(1)} %bitcast.119, f32[2048]{0:T(1024)S(1)} %bitcast.121, f32[2048]{0:T(1024)S(1)} %bitcast.123, ...), kind=kLoop, calls=%fused_computation.201 | loop fusion | flops 70254592 | bytes 140780032 | tf_op jit(solution)/shard_map/convert_element_type | solution.py:88
  94.2 5.3 %fusion.177 = f32[512,1024]{1,0:T(8,128)} fusion(bf16[512,2048]{1,0:T(8,128)(2,1)} %fusion.132, bf16[2048,1024]{1,0:T(8,128)(2,1)S(1)} %copy-done.9), kind=kOutput, calls=%fused_computation.289 | convolution fusion | flops 2147483648 | bytes 8388608 | tf_op jit(solution)/shard_map/dot_general | solution.py:89
  99.6 0.3 all-reduce.6.cloned.1.call-start
  99.9 12.5 %fusion.129 = (f32[2048]{0:T(1024)S(1)}, f32[2048]{0:T(1024)S(1)}, f32[2048]{0:T(1024)S(1)}, f32[2048]{0:T(1024)S(1)}, f32[2048]{0:T(1024)S(1)}, /*index=5*/f32[2048]{0:T(1024)S(1)}) fusion(f32[32,2048]{1,0:T(8,128)S(1)} %collective-permute-done, f32[512,2048]{1,0:T(8,128)} %copy-done.3, f32[544,2048]{1,0:T(8,128)} %copy-done.1), kind=kLoop, calls=%fused_computation.197 | loop fusion | flops 18862080 | bytes 8699904 | tf_op jit(solution)/shard_map/reduce_sum | solution.py:97
  112.6 3.8 %fusion.78 = (f32[2048]{0:T(1024)S(1)}, f32[2048]{0:T(1024)S(1)}, f32[2048]{0:T(1024)S(1)}, f32[2048]{0:T(1024)S(1)}, f32[2048]{0:T(1024)S(1)}, /*index=5*/f32[2048]{0:T(1024)S(1)}) fusion(f32[32,2048]{1,0:T(8,128)S(1)} %collective-permute-done.1, f32[512,2048]{1,0:T(8,128)S(1)} %copy-done.5, f32[544,2048]{1,0:T(8,128)S(1)} %copy-done.2), kind=kLoop, calls=%fused_computation.146 | loop fusion | flops 18862080 | bytes 8699904 | tf_op jit(solution)/shard_map/reduce_sum | solution.py:97
  116.4 3.8 %fusion.81 = (f32[2048]{0:T(1024)S(1)}, f32[2048]{0:T(1024)S(1)}, f32[2048]{0:T(1024)S(1)}, f32[2048]{0:T(1024)S(1)}, f32[2048]{0:T(1024)S(1)}, /*index=5*/f32[2048]{0:T(1024)S(1)}) fusion(f32[32,2048]{1,0:T(8,128)S(1)} %collective-permute-done.1, f32[512,2048]{1,0:T(8,128)S(1)} %copy-done.5, f32[544,2048]{1,0:T(8,128)S(1)} %copy-done.2), kind=kLoop, calls=%fused_computation.149 | loop fusion | flops 18862080 | bytes 8699904 | tf_op jit(solution)/shard_map/reduce_sum | solution.py:97
  120.2 3.2 fusion.126
  123.4 5.4 %fusion.75 = (f32[2048]{0:T(1024)S(1)}, f32[2048]{0:T(1024)S(1)}, f32[2048]{0:T(1024)S(1)}, f32[2048]{0:T(1024)S(1)}, f32[2048]{0:T(1024)S(1)}, /*index=5*/f32[2...) fusion(f32[32,2048]{1,0:T(8,128)S(1)} %collective-permute-done.1, f32[512,2048]{1,0:T(8,128)S(1)} %copy-done.5, ...), kind=kLoop, calls=%fused_computation.143 | loop fusion | flops 27244544 | bytes 8986624 | tf_op jit(solution)/shard_map/reduce_sum | solution.py:97
  128.8 3.5 %stack.135 = f32[33,2048]{1,0:T(8,128)} concatenate(f32[1,2048]{1,0:T(1,128)S(1)} %bitcast.162, f32[1,2048]{1,0:T(1,128)S(1)} %bitcast.163, f32[1,2048]{1,0:T(1,128)S(1)} %bitcast.164, f32[1,2048]{1,0:T(1,128)S(1)} %bitcast.165, f32[1,2048]{1,0:T(1,128)S(1)} %bitcast.166, f32[1,2048]{1,0:T(1,128)S(1)} %bitcast.180, f32[1,2048]{1,0:T(1,128)S(1)} %bitcast.181, ...), dimensions={0} | concatenate | bytes 540672 | tf_op jit(solution)/shard_map/stack | solution.py:95
  132.4 7.2 %fusion.164 = f32[2048,1024]{1,0:T(8,128)} fusion(bf16[512,2048]{1,0:T(8,128)(2,1)} %fusion.132, bf16[1,512,1024]{2,1,0:T(8,128)(2,1)S(1)} %copy-done), kind=kOutput, calls=%fused_computation.267 | convolution fusion | flops 2147483648 | bytes 11534336 | tf_op jit(solution)/shard_map/dot_general | solution.py:92
  139.6 2.1 fusion.167
  141.8 172.5 %all-reduce.6.cloned.1.call-done = (f32[2048,1024]{1,0:T(8,128)}, f32[33,2048]{1,0:T(8,128)}) async-done(((f32[2048,1024]{1,0:T(8,128)}, f32[33,2048]{1,0:T(8,128)}), (f32[2048,1024]{1,0:T(8,128)}, f32[33,2048]{1,0:T(8,128)})) %all-reduce.6.cloned.1.call-update) | async-done | bytes 8658960 | tf_op jit(solution)/shard_map/psum | solution.py:101
  314.2 2.7 multiply_convert_fusion
  317.0 1.7 copy.13
  (36 shorter events, 0.8 us)
Async XLA Ops:
  8.0 7.8 %copy-start = (bf16[1,512,1024]{2,1,0:T(8,128)(2,1)S(1)}, bf16[1,512,1024]{2,1,0:T(8,128)(2,1)}, u32[]{:S(2)}) copy-start(bf16[1,512,1024]{2,1,0:T(8,128)(2,1)} %param.5) | copy-start | bytes 3145732
  8.0 131.6 %reduce-scatter.2.cloned.1.call-start = ((), (), s32[]{:S(2)}) async-start(), calls=%async_computation.1 | async-start | bytes 3145728 | tf_op jit(solution)/shard_map/reduce_scatter | solution.py:90
  8.9 21.0 %collective-permute-start.2 = (s32[16]{0:T(128)S(1)}, s32[16]{0:T(128)S(1)}, u32[]{:S(2)}, u32[]{:S(2)}) collective-permute-start(s32[16]{0:T(128)S(1)} %get-tuple-element.101), channel_id=1, source_target_pairs={{0,8},{8,16},{16,24},{1,9},{9,17},{17,25},{2,10},{10,18},{18,26},{... | collective-permute-start | bytes 200 | tf_op jit(solution)/shard_map/ppermute | solution.py:25
  13.8 16.0 %collective-permute-start.3 = (s32[16]{0:T(128)S(1)}, s32[16]{0:T(128)S(1)}, u32[]{:S(2)}, u32[]{:S(2)}) collective-permute-start(s32[16]{0:T(128)S(1)} %get-tuple-element.102), channel_id=1, source_target_pairs={{8,0},{16,8},{24,16},{9,1},{17,9},{25,17},{10,2},{18,10},{26,18},{... | collective-permute-start | bytes 200 | tf_op jit(solution)/shard_map/ppermute | solution.py:26
  15.8 12.5 %copy-start.7 = (f32[33,2048]{1,0:T(8,128)S(1)}, f32[33,2048]{1,0:T(8,128)}, u32[]{:S(2)}) copy-start(f32[33,2048]{1,0:T(8,128)} %param.7) | copy-start | bytes 811012
  15.8 12.8 %copy-start.10 = (u32[32]{0:T(128)S(1)}, u32[32]{0:T(128)}, u32[]{:S(2)}) copy-start(u32[32]{0:T(128)} %constant.48) | copy-start | bytes 388
  15.8 14.0 %copy-start.8 = (s32[1,512]{1,0:T(1,128)S(1)}, s32[1,512]{1,0:T(1,128)}, u32[]{:S(2)}) copy-start(s32[1,512]{1,0:T(1,128)} %param.8) | copy-start | bytes 6148
  20.5 2.0 copy-start.3
  22.5 9.5 %collective-permute-start = (f32[32,2048]{1,0:T(8,128)S(1)}, f32[32,2048]{1,0:T(8,128)S(1)}, u32[]{:S(2)}, u32[]{:S(2)}) collective-permute-start(f32[32,2048]{1,0:T(8,128)S(1)} %get-tuple-element.66), channel_id=1, source_target_pairs={{0,8},{8,16},{16,24},{1,9},{9,17},{17,25},{2,10},{10,18},{18,26},{... | collective-permute-start | bytes 786440 | tf_op jit(solution)/shard_map/ppermute | solution.py:25
  27.0 9.1 %collective-permute-start.1 = (f32[32,2048]{1,0:T(8,128)S(1)}, f32[32,2048]{1,0:T(8,128)S(1)}, u32[]{:S(2)}, u32[]{:S(2)}) collective-permute-start(f32[32,2048]{1,0:T(8,128)S(1)} %get-tuple-element.67), channel_id=1, source_target_pairs={{8,0},{16,8},{24,16},{9,1},{17,9},{25,17},{10,2},{18,10},{26,18},{... | collective-permute-start | bytes 786440 | tf_op jit(solution)/shard_map/ppermute | solution.py:26
  29.9 9.0 %copy-start.4 = (f32[512,2048]{1,0:T(8,128)S(1)}, f32[512,2048]{1,0:T(8,128)}, u32[]{:S(2)}) copy-start(f32[512,2048]{1,0:T(8,128)} %copy-done.3) | copy-start | bytes 12582916
  61.2 2.0 copy-start.6
  75.8 18.4 %copy-start.1 = (f32[544,2048]{1,0:T(8,128)}, f32[544,2048]{1,0:T(8,128)S(1)}, u32[]{:S(2)}) copy-start(f32[544,2048]{1,0:T(8,128)S(1)} %subtract_select_fusion) | copy-start | bytes 13369348
  75.8 18.4 %copy-start.9 = (bf16[2048,1024]{1,0:T(8,128)(2,1)S(1)}, bf16[2048,1024]{1,0:T(8,128)(2,1)}, u32[]{:S(2)}) copy-start(bf16[2048,1024]{1,0:T(8,128)(2,1)} %param.6) | copy-start | bytes 12582916
  99.6 214.7 %all-reduce.6.cloned.1.call-start = ((), (), s32[]{:S(2)}) async-start(), calls=%async_computation.2 | async-start | bytes 17432576 | tf_op jit(solution)/shard_map/psum | solution.py:101
  99.8 12.5 %copy-start.2 = (f32[544,2048]{1,0:T(8,128)S(1)}, f32[544,2048]{1,0:T(8,128)}, u32[]{:S(2)}) copy-start(f32[544,2048]{1,0:T(8,128)} %copy-done.1) | copy-start | bytes 13369348
  99.8 12.7 %copy-start.5 = (f32[512,2048]{1,0:T(8,128)S(1)}, f32[512,2048]{1,0:T(8,128)}, u32[]{:S(2)}) copy-start(f32[512,2048]{1,0:T(8,128)} %copy-done.3) | copy-start | bytes 12582916
Sparse Core Ops, SparseCore 0:
  99.7 31.1 reduce-scatter.1
Sparse Core Ops, SparseCore 1:
  139.7 174.5 all-reduce.5
where the time goes:
time: 327 us; the launch traced here: 326 us
  waiting for transfers between devices  179 us (55%)
  other arithmetic  81 us (25%)
  matrix products  17.1 us (5%)
  between operations  17.1 us (5%)
  starting transfers between devices  12.4 us (4%)
  local copies, waits for them, and re-layouts  11.7 us (4%)
  blocking collectives  8.1 us (2%)
    psum x1, waiting for transfers between devices, per_device(): lax.psum((query_part, kernel_part), ('tm', 'rec'))  172 us
    reduce_sum x5, other arithmetic, per_device(): jnp.sum(map_grad * padded[offset:offset + row_count], axis=0)  28.7 us
    reduce_max x1, other arithmetic, row_softmax(): local_top = jnp.max(smooth, axis=1)  22.3 us
    convert_element_type x1, other arithmetic, per_device(): jnp.where(is_valid[:, None], score_grad, 0.0).astype(jnp.bfloat16)  18.4 us
    ppermute x2, starting transfers between devices, with_halo(): before = lax.ppermute(last, axis, up)  9.51 us
    unnamed x1, blocking collectives  8.1 us
    dot_general x1, matrix products, per_device(): lax.dot_general(score_grad, frame_rows, (((0,), (0,)), ((), ())), preferr...  7.19 us
    unnamed x28, local copies, waits for them, and re-layouts  7.14 us
  transfers between devices with their start and end apart: 6, of which 3 were waited for; matrix products, arithmetic and copies ran while one was open for 14% of the time, Pallas kernels for 0%

commit v1 on v0

--- a/solution.py
+++ b/solution.py
@@ -98,7 +98,7 @@
             for offset in range(tap_count)
         ]
     )
-    query_whole, grad_kernel = lax.psum((query_part, kernel_part), ("tm", "rec"))
+    query_whole, grad_kernel = lax.psum(lax.psum((query_part, kernel_part), "rec"), "tm")
     col_count = width // lax.axis_size("rec")
     query_cols = lax.dynamic_slice_in_dim(
         query_whole, lax.axis_index("rec") * col_count, col_count, 1

time: 327 us -> 596 us (1.82)
  waiting for transfers between devices: 179 us -> 458 us
  other arithmetic: 81 us -> 71 us
    psum x1 -> x2, waiting for transfers between devices: 172 us -> 452 us  [the longest x1 302 us: per_device(): lax.psum(lax.psum((query_part, kernel_part), 'rec'), 'tm')]
    reduce_sum x5, other arithmetic: 28.7 us -> 19.4 us  [per_device(): jnp.sum(map_grad * padded[offset:offset + row_count], axis=0)]
  transfers between devices with their start and end apart: 6 -> 7, of which waited for: 3 -> 4; matrix products, arithmetic and copies ran while one was open for 14% -> 2% of each run, Pallas kernels for 0% -> 0%
where the time goes in v1:
time: 596 us
  waiting for transfers between devices  458 us (77%)
  other arithmetic  71 us (12%)
  between operations  17.1 us (3%)
  matrix products  16.1 us (3%)
  local copies, waits for them, and re-layouts  13 us (2%)
  starting transfers between devices  12.2 us (2%)
  blocking collectives  8.09 us (1%)
    psum x1, waiting for transfers between devices, per_device(): lax.psum(lax.psum((query_part, kernel_part), 'rec'), 'tm')  302 us
    psum x1, waiting for transfers between devices, per_device(): lax.psum((query_part, kernel_part), 'rec')  150 us
    reduce_max x1, other arithmetic, row_softmax(): local_top = jnp.max(smooth, axis=1)  22.3 us
    reduce_sum x5, other arithmetic, per_device(): jnp.sum(map_grad * padded[offset:offset + row_count], axis=0)  19.4 us
    convert_element_type x1, other arithmetic, per_device(): jnp.where(is_valid[:, None], score_grad, 0.0).astype(jnp.bfloat16)  17.6 us
  transfers between devices with their start and end apart: 7, of which 4 were waited for; matrix products, arithmetic and copies ran while one was open for 2% of the time, Pallas kernels for 0%

profile of v1, /device:TPU:0, one launch (start us, length us, event | category | flops | bytes accessed | tf_op | source)
XLA Modules:
  0.0 595.9 jit_solution(15466997710117592334)
XLA Ops:
  8.1 0.8 slice_bitcast_fusion.1
  8.9 4.9 collective-permute-start.2
  13.8 1.3 collective-permute-start.3
  15.8 4.6 multiply_select_fusion
  20.5 1.9 copy-done.1
  22.4 4.6 collective-permute-start
  27.0 1.3 collective-permute-start.1
  28.6 0.6 dynamic-slice
  29.9 2.1 collective-permute-done
  32.0 4.1 collective-permute-done.1
  36.1 2.8 pad_maximum_fusion.2
  38.9 22.3 %fusion.172 = (f32[544]{0:T(1024)S(1)}, f32[544,2048]{1,0:T(8,128)S(1)}) fusion(f32[32,2048]{1,0:T(8,128)S(1)} %collective-permute-done.1, f32[512,2048]{1,0:T(8,128)S(1)} %copy-done.2, f32[2048]{0:T(1024)S(1)} %bitcast.110, f32[576,2048]{1,0:T(8,128)S(1)} %pad_maximum_fusion.2, f32[2048]{0:T(1024)S(1)} %bitcast.112, f32[2048]{0:T(1024)S(1)} %bitcast.116, ...), kind=kLoop, calls=%fused_computation.285 | loop fusion | flops 75759072 | bytes 147597440 | tf_op jit(solution)/shard_map/reduce_max | solution.py:49
  61.2 2.0 copy-done.4
  63.2 0.7 exponential_reduce_fusion
  63.9 0.3 dynamic-update-slice
  64.5 8.1 %all-reduce.4 = (f32[1088]{0:T(1024)S(1)}, f32[1088]{0:T(1024)S(1)}) all-reduce(f32[1088]{0:T(1024)S(1)} %dynamic-update-slice.1, f32[1088]{0:T(1024)S(1)} %dynamic-update-slice), channel_id=3, replica_groups=mesh['tm'=4,'query'=2,'rec'=4] {'query'}, use_global_device_ids=true, to_apply=%add.1 | all-reduce | flops 2176 | bytes 17408
  72.7 3.1 subtract_select_fusion
  75.8 17.6 %fusion.132 = bf16[512,2048]{1,0:T(8,128)(2,1)S(1)} fusion(f32[544,2048]{1,0:T(8,128)S(1)} %subtract_select_fusion, f32[2048]{0:T(1024)S(1)} %bitcast.111, f32[2048]{0:T(1024)S(1)} %bitcast.113, f32[2048]{0:T(1024)S(1)} %bitcast.117, f32[2048]{0:T(1024)S(1)} %bitcast.119, f32[2048]{0:T(1024)S(1)} %bitcast.121, f32[2048]{0:T(1024)S(1)} %bitcast.123, ...), kind=kLoop, calls=%fused_computation.201 | loop fusion | flops 70254592 | bytes 140780032 | tf_op jit(solution)/shard_map/convert_element_type | solution.py:88
  93.5 5.6 fusion.164
  99.1 3.2 fusion.129
  102.3 3.8 fusion.78
  106.1 3.8 fusion.81
  110.0 5.4 fusion.75
  115.4 3.2 fusion.126
  118.6 3.5 stack.135
  122.2 1.5 copy-done.6
  123.7 5.9 fusion.177
  129.7 150.1 %all-reduce.8.cloned.1.call-done = (f32[2048,1024]{1,0:T(8,128)}, f32[33,2048]{1,0:T(8,128)}) async-done(((f32[2048,1024]{1,0:T(8,128)}, f32[33,2048]{1,0:T(8,128)}), (f32[2048,1024]{1,0:T(8,128)}, f32[33,2048]{1,0:T(8,128)})) %all-reduce.8.cloned.1.call-update) | async-done | bytes 8658960 | tf_op jit(solution)/shard_map/psum | solution.py:101
  279.8 2.1 fusion.167
  281.9 302.0 %all-reduce.10.cloned.1.call-done = (f32[2048,1024]{1,0:T(8,128)}, f32[33,2048]{1,0:T(8,128)}) async-done(((f32[2048,1024]{1,0:T(8,128)}, f32[33,2048]{1,0:T(8,128)}), (f32[2048,1024]{1,0:T(8,128)}, f32[33,2048]{1,0:T(8,128)})) %all-reduce.10.cloned.1.call-update) | async-done | bytes 8658960 | tf_op jit(solution)/shard_map/psum | solution.py:101
  584.0 2.7 multiply_convert_fusion
  586.7 1.7 copy.15
  (37 shorter events, 0.9 us)
Async XLA Ops:
  8.0 7.8 %copy-start = (bf16[1,512,1024]{2,1,0:T(8,128)(2,1)S(1)}, bf16[1,512,1024]{2,1,0:T(8,128)(2,1)}, u32[]{:S(2)}) copy-start(bf16[1,512,1024]{2,1,0:T(8,128)(2,1)} %param.5) | copy-start | bytes 3145732
  8.0 271.7 %all-reduce.8.cloned.1.call-start = ((), (), s32[]{:S(2)}) async-start(), calls=%async_computation.2 | async-start | bytes 17432576 | tf_op jit(solution)/shard_map/psum | solution.py:101
  8.9 20.9 %collective-permute-start.2 = (s32[16]{0:T(128)S(1)}, s32[16]{0:T(128)S(1)}, u32[]{:S(2)}, u32[]{:S(2)}) collective-permute-start(s32[16]{0:T(128)S(1)} %get-tuple-element.103), channel_id=1, source_target_pairs={{0,8},{8,16},{16,24},{1,9},{9,17},{17,25},{2,10},{10,18},{18,26},{... | collective-permute-start | bytes 200 | tf_op jit(solution)/shard_map/ppermute | solution.py:25
  13.8 16.0 %collective-permute-start.3 = (s32[16]{0:T(128)S(1)}, s32[16]{0:T(128)S(1)}, u32[]{:S(2)}, u32[]{:S(2)}) collective-permute-start(s32[16]{0:T(128)S(1)} %get-tuple-element.104), channel_id=1, source_target_pairs={{8,0},{16,8},{24,16},{9,1},{17,9},{25,17},{10,2},{18,10},{26,18},{... | collective-permute-start | bytes 200 | tf_op jit(solution)/shard_map/ppermute | solution.py:26
  15.8 12.5 %copy-start.7 = (f32[33,2048]{1,0:T(8,128)S(1)}, f32[33,2048]{1,0:T(8,128)}, u32[]{:S(2)}) copy-start(f32[33,2048]{1,0:T(8,128)} %param.7) | copy-start | bytes 811012
  15.8 12.7 %copy-start.9 = (u32[32]{0:T(128)S(1)}, u32[32]{0:T(128)}, u32[]{:S(2)}) copy-start(u32[32]{0:T(128)} %constant.48) | copy-start | bytes 388
  15.8 14.0 %copy-start.8 = (s32[1,512]{1,0:T(1,128)S(1)}, s32[1,512]{1,0:T(1,128)}, u32[]{:S(2)}) copy-start(s32[1,512]{1,0:T(1,128)} %param.8) | copy-start | bytes 6148
  20.5 1.9 copy-start.1
  22.4 9.5 %collective-permute-start = (f32[32,2048]{1,0:T(8,128)S(1)}, f32[32,2048]{1,0:T(8,128)S(1)}, u32[]{:S(2)}, u32[]{:S(2)}) collective-permute-start(f32[32,2048]{1,0:T(8,128)S(1)} %get-tuple-element.68), channel_id=1, source_target_pairs={{0,8},{8,16},{16,24},{1,9},{9,17},{17,25},{2,10},{10,18},{18,26},{... | collective-permute-start | bytes 786440 | tf_op jit(solution)/shard_map/ppermute | solution.py:25
  27.0 9.1 %collective-permute-start.1 = (f32[32,2048]{1,0:T(8,128)S(1)}, f32[32,2048]{1,0:T(8,128)S(1)}, u32[]{:S(2)}, u32[]{:S(2)}) collective-permute-start(f32[32,2048]{1,0:T(8,128)S(1)} %get-tuple-element.69), channel_id=1, source_target_pairs={{8,0},{16,8},{24,16},{9,1},{17,9},{25,17},{10,2},{18,10},{26,18},{... | collective-permute-start | bytes 786440 | tf_op jit(solution)/shard_map/ppermute | solution.py:26
  29.9 9.0 %copy-start.2 = (f32[512,2048]{1,0:T(8,128)S(1)}, f32[512,2048]{1,0:T(8,128)}, u32[]{:S(2)}) copy-start(f32[512,2048]{1,0:T(8,128)} %copy-done.1) | copy-start | bytes 12582916
  61.1 2.0 copy-start.4
  93.4 5.7 copy-start.5
  93.5 5.7 copy-start.3
  122.1 1.6 copy-start.6
  122.2 157.6 %reduce-scatter.2.cloned.1.call-start = ((), (), s32[]{:S(2)}) async-start(), calls=%async_computation.1 | async-start | bytes 3145728 | tf_op jit(solution)/shard_map/reduce_scatter | solution.py:90
  129.6 454.3 %all-reduce.10.cloned.1.call-start = ((), (), s32[]{:S(2)}) async-start(), calls=%async_computation.3 | async-start | bytes 17432576 | tf_op jit(solution)/shard_map/psum | solution.py:101
Sparse Core Ops, SparseCore 0:
  122.3 157.4 all-reduce.7
  282.4 301.5 all-reduce.9
Sparse Core Ops, SparseCore 1:
  129.7 31.1 reduce-scatter.1
